TPU v7x, 512 devices: a whole 4x8x8 slice. The times are simulated.
512 devices in a mesh: dp: 32 (over x, y), expert: 16 (over z, core).
Axes of the slice: x: 4, y: 8, z: 8, core: 2. Of those that a mesh axis runs over, the one named last changes fastest.
Arguments:
- tokens: bfloat16 [8192, 2048], P('expert', 'dp'), may hold values from -6 to 6
- routes: int32 [8192, 2], P('expert'), may hold values from 0 to 15, all different within a row; in each aligned block of 512 rows (0 to 511, 512 to 1023, ...) at most 96 rows name the same one
- scores: int32 [8192, 2], P('expert'), may hold values from 1 to 1023
- gate_weight: bfloat16 [16, 2048, 8192], P('expert', None, 'dp'), may hold values from -0.125 to 0.125
- up_weight: bfloat16 [16, 2048, 8192], P('expert', None, 'dp'), may hold values from -0.125 to 0.125
- down_weight: bfloat16 [16, 8192, 2048], P('expert', 'dp'), may hold values from -0.0625 to 0.0625
Outputs:
- layer_out: bfloat16 [8192, 2048], P('expert', 'dp')
Inputs may be any that keep to these rules, and one draw needn't show every extreme that they name: `routes`: each row names 2 different experts. Within each aligned block of 512 rows no expert is named by more than 96 rows, and in every draw some expert is named by exactly 96 rows of a block.
All inputs are finite; a program needn't handle non-finite values.
Results may differ from a plain program's by a relative error of at most 0.025.
Values may be sent and summed in bfloat16 or wider, within the bound.
A program may use at most 64 MiB of HBM per device.

v0:
```python
import jax
import jax.numpy as jnp
from jax import lax
from jax.sharding import PartitionSpec as P


def shards(tokens, routes, scores, gate_weight, up_weight, down_weight):
    expert_count = lax.axis_size("expert")
    row_count = tokens.shape[0]
    local_cols = tokens.shape[1]
    capacity = 3 * row_count // expert_count
    slot_count = expert_count * capacity
    expert_ids = jnp.arange(expert_count, dtype=jnp.int32)
    onehot = (routes[:, :, None] == expert_ids[None, None, :]).astype(jnp.int32)
    named = jnp.sum(onehot, axis=1)
    earlier = jnp.cumsum(named, axis=0) - named
    slot_rank = jnp.sum(onehot * earlier[:, None, :], axis=2)
    target = routes * capacity + slot_rank
    slot_ids = jnp.arange(slot_count, dtype=jnp.int32)
    placement = jnp.any(target[None, :, :] == slot_ids[:, None, None], axis=2).astype(jnp.bfloat16)
    weight = scores.astype(jnp.float32)
    weight = weight / jnp.sum(weight, axis=1, keepdims=True)
    gate_mat = gate_weight[0]
    up_mat = up_weight[0]
    down_mat = down_weight[0]
    outgoing = jnp.dot(placement, tokens, preferred_element_type=jnp.float32).astype(jnp.bfloat16)
    arrived = lax.all_to_all(
        outgoing.reshape(expert_count, capacity, local_cols),
        "expert",
        split_axis=0,
        concat_axis=0,
        tiled=True,
    )
    arrived = arrived.reshape(slot_count, local_cols)
    piece = lax.all_gather(arrived, "dp", axis=1, tiled=True)
    gate = jnp.dot(piece, gate_mat, preferred_element_type=jnp.float32)
    upval = jnp.dot(piece, up_mat, preferred_element_type=jnp.float32)
    hidden = (jax.nn.silu(gate) * upval).astype(jnp.bfloat16)
    summed = lax.psum_scatter(
        lax.dot_general(
            down_mat, hidden, (((0,), (1,)), ((), ())), preferred_element_type=jnp.float32
        ).astype(jnp.bfloat16),
        "dp",
        scatter_dimension=0,
        tiled=True,
    ).astype(jnp.float32)
    returned = lax.all_to_all(
        summed.reshape(local_cols, expert_count, capacity).astype(jnp.bfloat16),
        "expert",
        split_axis=1,
        concat_axis=1,
        tiled=True,
    ).astype(jnp.float32)
    returned = returned.reshape(local_cols, slot_count)
    first_part = jnp.take(returned, target[:, 0], axis=1)
    second_part = jnp.take(returned, target[:, 1], axis=1)
    combined = (first_part * weight[:, 0][None, :] + second_part * weight[:, 1][None, :]).T
    return combined.astype(jnp.bfloat16)


def solution(mesh):
    return jax.shard_map(
        shards,
        mesh=mesh,
        in_specs=(
            P("expert", "dp"),
            P("expert", None),
            P("expert", None),
            P("expert", None, "dp"),
            P("expert", None, "dp"),
            P("expert", "dp", None),
        ),
        out_specs=P("expert", "dp"),
        check_vma=False,
    )
```

profile of v0, /device:TPU:1, one launch (start us, length us, event | category | flops | bytes accessed | tf_op | source)
XLA Modules:
  0.0 414.6 jit_solution(14097522096676943779)
XLA Ops:
  6.5 0.8 convert_reduce_fusion
  7.3 1.2 reduce-window.6
  8.5 0.2 slice_reduce_fusion
  8.8 0.1 fusion.12
  8.8 0.7 select_reduce_fusion
  9.6 0.7 multiply_add_fusion
  10.3 2.0 fusion.1
  12.2 1.4 convolution_convert_fusion.1
  13.7 0.2 reshape.37
  13.9 0.1 copy.37
  14.0 23.3 %all_to_all.10 = bf16[16,96,64]{1,2,0:T(8,128)(2,1)S(1)} all-to-all(bf16[16,96,64]{1,2,0:T(8,128)(2,1)S(1)} %copy.37), channel_id=1, replica_groups=mesh['dp'=32,'expert'=16] {'expert'}, dimensions={0} | all-to-all | bytes 393216 | tf_op jit(solution)/shard_map/all_to_all | solution.py:27
  37.3 0.2 copy.38
  37.5 0.9 reshape.38
  38.5 0.0 all-gather.2.cloned.1.call-update
  38.5 0.0 copy-start.2
  38.5 0.0 reduce-scatter.4.cloned.1.call-start
  38.5 89.9 %all-gather.2.cloned.1.call-done = bf16[1536,2048]{0,1:T(8,128)(2,1)} async-done(((bf16[1536,64]{0,1:T(8,128)(2,1)}), bf16[1536,2048]{0,1:T(8,128)(2,1)}) %all-gather.2.cloned.1.call-update) | async-done | bytes 6291472 | tf_op jit(solution)/shard_map/all_gather | solution.py:35
  128.4 6.1 %fusion.6 = f32[1536,256]{1,0:T(8,128)} fusion(bf16[1536,2048]{0,1:T(8,128)(2,1)} %all-gather.2.cloned.1.call-done, bf16[1,2048,256]{2,1,0:T(8,128)(2,1)} %param.11), kind=kOutput, calls=%fused_computation.11 | convolution fusion | flops 1610612736 | bytes 8912896 | tf_op jit(solution)/shard_map/dot_general | solution.py:36
  134.5 12.3 %fusion = bf16[2048,1536]{0,1:T(8,128)(2,1)} fusion(bf16[1536,2048]{0,1:T(8,128)(2,1)} %all-gather.2.cloned.1.call-done, f32[1536,256]{1,0:T(8,128)} %fusion.6, bf16[1,256,2048]{2,1,0:T(8,128)(2,1)S(1)} %copy-done, bf16[1,2048,256]{2,1,0:T(8,128)(2,1)S(1)} %copy-done.2), kind=kOutput, calls=%fused_computation.3 | convolution fusion | flops 3226730496 | bytes 16252928 | tf_op jit(solution)/shard_map/dot_general | solution.py:40
  146.8 8.7 %copy.42 = bf16[2048,1536]{1,0:T(8,128)(2,1)} copy(bf16[2048,1536]{0,1:T(8,128)(2,1)} %fusion) | data formatting | bytes 12582912
  155.5 0.0 reduce-scatter.4.cloned.1.call-update
  155.5 0.7 copy-done.1
  156.3 222.8 %reduce-scatter.4.cloned.1.call-done = bf16[64,1536]{1,0:T(8,128)(2,1)} async-done(((bf16[2048,1536]{1,0:T(8,128)(2,1)}), bf16[64,1536]{1,0:T(8,128)(2,1)}) %reduce-scatter.4.cloned.1.call-update) | async-done | bytes 196624
  379.0 1.1 copy.43
  380.2 0.9 copy.39
  381.0 11.6 %all-to-all-start.1 = ((bf16[64,16,96]{2,0,1:T(8,128)(2,1)}), bf16[64,16,96]{2,0,1:T(8,128)(2,1)S(1)}, u32[]{:S(2)}, u32[]{:S(2)}) async-start(bf16[64,16,96]{2,0,1:T(8,128)(2,1)} %copy.39), calls=%async_computation.1 | async-start | bytes 524288 | tf_op jit(solution)/shard_map/all_to_all | solution.py:47
  392.7 11.7 %all-to-all-done.1 = bf16[64,16,96]{2,0,1:T(8,128)(2,1)S(1)} async-done(((bf16[64,16,96]{2,0,1:T(8,128)(2,1)}), bf16[64,16,96]{2,0,1:T(8,128)(2,1)S(1)}, u32[]{:S(2)}, u32[]{:S(2)}) %all-to-all-start.1) | async-done | bytes 196640 | tf_op jit(solution)/shard_map/all_to_all | solution.py:47
  404.4 0.2 copy.40
  404.6 1.0 gather_fusion
  405.6 1.0 gather_fusion.1
  406.6 0.3 fusion.11
  407.0 0.7 copy.41
  (17 shorter events, 0.1 us)
Async XLA Ops:
  6.5 128.0 %copy-start = (bf16[1,256,2048]{2,1,0:T(8,128)(2,1)S(1)}, bf16[1,256,2048]{2,1,0:T(8,128)(2,1)}, u32[]{:S(2)}) copy-start(bf16[1,256,2048]{2,1,0:T(8,128)(2,1)} %param.13) | copy-start | bytes 3145732
  6.5 121.9 %all-gather.2.cloned.1.call-start = ((), (), s32[]{:S(2)}) async-start(), calls=%async_computation.3 | async-start | bytes 6488064 | tf_op jit(solution)/shard_map/all_gather | solution.py:35
  38.5 96.0 %copy-start.2 = (bf16[1,2048,256]{2,1,0:T(8,128)(2,1)S(1)}, bf16[1,2048,256]{2,1,0:T(8,128)(2,1)}, u32[]{:S(2)}) copy-start(bf16[1,2048,256]{2,1,0:T(8,128)(2,1)} %param.12) | copy-start | bytes 3145732
  38.5 340.5 %reduce-scatter.4.cloned.1.call-start = ((), (), s32[]{:S(2)}) async-start(), calls=%async_computation.4 | async-start | bytes 6488064
  155.5 0.7 copy-start.1
  381.0 23.3 %all-to-all-start.1 = ((bf16[64,16,96]{2,0,1:T(8,128)(2,1)}), bf16[64,16,96]{2,0,1:T(8,128)(2,1)S(1)}, u32[]{:S(2)}, u32[]{:S(2)}) async-start(bf16[64,16,96]{2,0,1:T(8,128)(2,1)} %copy.39), calls=%async_computation.1 | async-start | bytes 524288 | tf_op jit(solution)/shard_map/all_to_all | solution.py:47
Sparse Core Ops, SparseCore 0:
  38.6 89.7 all-gather.1
  155.6 223.3 reduce-scatter.3
where the time goes:
time: 415 us
  waiting for transfers between devices  324 us (78%)
  blocking collectives  23.3 us (6%)
  matrix products  19.8 us (5%)
  local copies, waits for them, and re-layouts  16 us (4%)
  between operations  13.5 us (3%)
  starting transfers between devices  11.7 us (3%)
  other arithmetic  5.85 us (1%)
    unnamed x3, waiting for transfers between devices  223 us
    all_gather x1, waiting for transfers between devices, shards(): piece = lax.all_gather(arrived, 'dp', axis=1, tiled=True)  89.9 us
    all_to_all x1, blocking collectives, shards(): lax.all_to_all(outgoing.reshape(expert_count, capacity, local_cols), 'exp...  23.3 us
    dot_general x1, matrix products, shards(): lax.dot_general(down_mat, hidden, (((0,), (1,)), ((), ())), preferred_ele...  12.3 us
    all_to_all x1, waiting for transfers between devices, shards(): lax.all_to_all(summed.reshape(local_cols, expert_count, capacity).astype(...  11.7 us
    all_to_all x1, starting transfers between devices, shards(): lax.all_to_all(summed.reshape(local_cols, expert_count, capacity).astype(...  11.6 us
    unnamed x8, local copies, waits for them, and re-layouts  10.5 us
  transfers between devices with their start and end apart: 3, of which 3 were waited for; matrix products, arithmetic and copies ran while one was open for 0% of the time, Pallas kernels for 0%

commit v1 on v0

v1 whole, which is shorter than its diff:
```python
import functools

import jax
import jax.numpy as jnp
from jax import lax
from jax.experimental import pallas as pl
from jax.experimental.pallas import tpu as pltpu
from jax.sharding import PartitionSpec as P

MESH = pl.DeviceIdType.MESH
NX, NY = 4, 8
LANES = 128
BF, F32 = jnp.bfloat16, jnp.float32


def moe_kernel(
    tokens_ref, routes_ref, scores_ref, gate_hbm, up_hbm, down_hbm, out_ref,
    gate_raw, up_raw, down_raw, gu_t, down_t, sel, disp_out, disp_in,
    x_buf, acc, hid, o_buf, r_main, r_turn, ret_out, ret_in, pick0, pick1,
    load_sem, disp_send, disp_recv, ag_send, ag_recv, rs_send, rs_recv, turn_recv, ret_send, ret_recv,
):
    n_exp = disp_in.shape[0]
    rows, width = tokens_ref.shape
    group = n_exp // 4
    span = x_buf.shape[3]
    cap = span // group
    hidden = gate_raw.shape[3]
    dp = lax.axis_index("dp")
    me = lax.axis_index("expert")
    x, y = dp // NY, dp % NY

    def at_xy(px, py):
        return (lax.rem(px + NX, NX) * NY + lax.rem(py + NY, NY), me)

    loads = [
        pltpu.make_async_copy(src, dst, load_sem.at[i])
        for i, (src, dst) in enumerate(((gate_hbm, gate_raw), (up_hbm, up_raw), (down_hbm, down_raw)))
    ]
    for load in loads:
        load.start()

    barrier = pltpu.get_barrier_semaphore()
    for target in (at_xy(x + 1, y), at_xy(x - 1, y), at_xy(x, y + 1), at_xy(x, y - 1)):
        pl.semaphore_signal(barrier, inc=1, device_id=target, device_id_type=MESH)
    for p in range(1, n_exp):
        pl.semaphore_signal(barrier, inc=1, device_id=(dp, lax.rem(me + p, n_exp)), device_id_type=MESH)

    routes = routes_ref[...]
    first, second = routes[:, 0:1], routes[:, 1:2]
    lane = lax.broadcasted_iota(jnp.int32, (rows, LANES), 1)
    is_first = (lane == first).astype(F32)
    is_second = (lane == second).astype(F32)
    earlier_mask = (
        lax.broadcasted_iota(jnp.int32, (rows, rows), 1) < lax.broadcasted_iota(jnp.int32, (rows, rows), 0)
    ).astype(F32).astype(BF)
    earlier = jnp.dot(earlier_mask, (is_first + is_second).astype(BF), preferred_element_type=F32)
    rank0 = jnp.sum(is_first * earlier, axis=1, keepdims=True).astype(jnp.int32)
    rank1 = jnp.sum(is_second * earlier, axis=1, keepdims=True).astype(jnp.int32)
    slot0 = first * LANES + rank0
    slot1 = second * LANES + rank1

    tok = tokens_ref[...]
    wide = group * LANES
    for q in range(4):
        ids = lax.broadcasted_iota(jnp.int32, (rows, wide), 1) + q * wide
        p0 = (ids == slot0).astype(F32)
        p1 = (ids == slot1).astype(F32)
        pick0[:, q * wide:(q + 1) * wide] = p0.astype(BF)
        pick1[:, q * wide:(q + 1) * wide] = p1.astype(BF)
        packed = lax.dot_general(
            tok, (p0 + p1).astype(BF), (((0,), (0,)), ((), ())), preferred_element_type=F32
        ).astype(BF)
        for i in range(group):
            disp_out[q * group + i] = packed[:, i * LANES:(i + 1) * LANES]
    disp_in[me] = disp_out[me]

    pl.semaphore_wait(barrier, 4 + n_exp - 1)

    def disp_copy(dest, src):
        return pltpu.make_async_remote_copy(
            src_ref=disp_out.at[dest], dst_ref=disp_in.at[src], send_sem=disp_send, recv_sem=disp_recv.at[src],
            device_id=(dp, dest), device_id_type=MESH)

    for p in range(1, n_exp):
        disp_copy(lax.rem(me + p, n_exp), me).start()

    si = lax.broadcasted_iota(jnp.int32, (wide, span), 0)
    sl = lax.broadcasted_iota(jnp.int32, (wide, span), 1)
    rank_in = si % LANES
    sel[...] = ((sl == (si // LANES) * cap + rank_in) & (rank_in < cap)).astype(F32).astype(BF)

    for st in range(4):
        acc[st] = jnp.zeros(acc.shape[1:], F32)

    for load in loads:
        load.wait()

    @pl.loop(0, NY)
    def _(yy):
        g = gate_raw[:, yy].reshape(NX * width, hidden)
        u = up_raw[:, yy].reshape(NX * width, hidden)
        gu_t[yy, 0:hidden, :] = g.T
        gu_t[yy, hidden:2 * hidden, :] = u.T

    for c in range(NX * NY // 2):
        turned = down_raw[:, c * LANES:(c + 1) * LANES].T
        for h in range(2):
            xx, yy = (2 * c + h) // NY, (2 * c + h) % NY
            down_t[yy, xx * width:(xx + 1) * width, :] = turned[h * width:(h + 1) * width, :]

    streams = [(True, 1), (True, -1), (False, 1), (False, -1)]

    def where(sign, j, k):
        px = lax.rem(x - sign * j + 2 * NX, NX)
        py = lax.rem(y - sign * k + 2 * NY, NY)
        return px, py

    def piece(buf, st, sign, j, k):
        px, py = where(sign, j, k)
        return buf.at[st, py, pl.ds(pl.multiple_of(px * width, width), width)]

    def ag_copy(st, sign, j, k, along_x):
        ref = piece(x_buf, st, sign, j, k)
        return pltpu.make_async_remote_copy(
            src_ref=ref, dst_ref=ref, send_sem=ag_send.at[st],
            recv_sem=ag_recv.at[st, j + 1, k] if along_x else ag_recv.at[st, j, k + 1],
            device_id=at_xy(x + sign, y) if along_x else at_xy(x, y + sign), device_id_type=MESH)

    def ag_wait(st, sign, j, k):
        ref = piece(x_buf, st, sign, j, k)
        pltpu.make_async_copy(ref, ref, ag_recv.at[st, j, k]).wait()

    for st, (y_first, sign) in enumerate(streams):
        for s in range(st * group, (st + 1) * group):
            @pl.when(s != me)
            def _():
                pltpu.make_async_copy(disp_in.at[s], disp_in.at[s], disp_recv.at[s]).wait()
        packed = jnp.concatenate([disp_in[st * group + i] for i in range(group)], axis=1)
        x_buf[st, y, pl.ds(pl.multiple_of(x * width, width), width), :] = jnp.dot(
            packed, sel[...], preferred_element_type=F32).astype(BF)
        ag_copy(st, sign, 0, 0, True).start()
        ag_copy(st, sign, 0, 0, False).start()

    @pl.loop(1, NX + NY - 1)
    def _(r):
        for j in range(NX):
            k = r - j

            @pl.when((k >= 0) & (k < NY))
            def _():
                for st, (y_first, sign) in enumerate(streams):
                    ag_wait(st, sign, j, k)
                    if y_first:
                        if j < NX - 1:
                            ag_copy(st, sign, j, k, True).start()
                        if j == 0:
                            @pl.when(k < NY - 1)
                            def _():
                                ag_copy(st, sign, j, k, False).start()
                    else:
                        if j < NX - 1:
                            @pl.when(k == 0)
                            def _():
                                ag_copy(st, sign, j, k, True).start()

                        @pl.when(k < NY - 1)
                        def _():
                            ag_copy(st, sign, j, k, False).start()

        done = r - (NX - 1)

        @pl.when(done >= 0)
        def _():
            for st, (y_first, sign) in enumerate(streams):
                _, py = where(sign, 0, done)
                acc[st] += jnp.dot(gu_t[py], x_buf[st, py], preferred_element_type=F32)

    for st in range(4):
        gate = acc[st, 0:hidden, :]
        hid[st] = (gate / (1.0 + jnp.exp(-gate)) * acc[st, hidden:2 * hidden, :]).astype(BF)

    def rs_copy(st, sign, j, k, dst, sem, along_x):
        return pltpu.make_async_remote_copy(
            src_ref=piece(o_buf, st, sign, j, k), dst_ref=dst, send_sem=rs_send.at[st], recv_sem=sem,
            device_id=at_xy(x - sign, y) if along_x else at_xy(x, y - sign), device_id_type=MESH)

    def add_from(st, sign, j, k, ref, sem):
        pltpu.make_async_copy(ref, ref, sem).wait()
        own = piece(o_buf, st, sign, j, k)
        own[...] = (own[...].astype(F32) + ref[...].astype(F32)).astype(BF)

    @pl.loop(0, NX + NY - 1)
    def _(r):
        fresh = NY - 1 - r

        @pl.when(fresh >= 0)
        def _():
            for st, (y_first, sign) in enumerate(streams):
                _, py = where(sign, 0, fresh)
                o_buf[st, py] = jnp.dot(down_t[py], hid[st], preferred_element_type=F32).astype(BF)

        for j in range(NX - 1, -1, -1):
            k = NX + NY - 2 - r - j

            @pl.when((k >= 0) & (k < NY))
            def _():
                for st, (y_first, sign) in enumerate(streams):
                    main = piece(r_main, st, sign, j, k)
                    if y_first:
                        if j < NX - 1:
                            add_from(st, sign, j, k, main, rs_recv.at[st, j, k])
                        if j > 0:
                            rs_copy(st, sign, j, k, main, rs_recv.at[st, j - 1, k], True).start()
                        else:
                            @pl.when(k < NY - 1)
                            def _():
                                add_from(st, sign, j, k, r_turn.at[st, k], turn_recv.at[st, k])

                            @pl.when(k > 0)
                            def _():
                                rs_copy(st, sign, j, k, r_turn.at[st, k - 1], turn_recv.at[st, k - 1], False).start()
                    else:
                        @pl.when(k < NY - 1)
                        def _():
                            add_from(st, sign, j, k, main, rs_recv.at[st, j, k])

                        @pl.when(k > 0)
                        def _():
                            rs_copy(st, sign, j, k, main, rs_recv.at[st, j, k - 1], False).start()

                        @pl.when(k == 0)
                        def _():
                            if j < NX - 1:
                                add_from(st, sign, j, k, r_turn.at[st, j], turn_recv.at[st, j])
                            if j > 0:
                                rs_copy(st, sign, j, k, r_turn.at[st, j - 1], turn_recv.at[st, j - 1], True).start()

    def ret_copy(dest, src):
        return pltpu.make_async_remote_copy(
            src_ref=ret_out.at[dest], dst_ref=ret_in.at[src], send_sem=ret_send, recv_sem=ret_recv.at[src],
            device_id=(dp, dest), device_id_type=MESH)

    for st, (y_first, sign) in enumerate(streams):
        total = piece(o_buf, st, sign, 0, 0)[...]
        spread = lax.dot_general(
            total, sel[...], (((1,), (1,)), ((), ())), preferred_element_type=F32).astype(BF)
        for i in range(group):
            ret_out[st * group + i] = spread[:, i * LANES:(i + 1) * LANES]
    ret_in[me] = ret_out[me]
    for p in range(1, n_exp):
        ret_copy(lax.rem(me + p, n_exp), me).start()

    weight = scores_ref[...].astype(F32)
    weight = weight / (weight[:, 0:1] + weight[:, 1:2])
    part0 = jnp.zeros((rows, width), F32)
    part1 = jnp.zeros((rows, width), F32)
    for s in range(n_exp):
        @pl.when(s != me)
        def _():
            pltpu.make_async_copy(ret_in.at[s], ret_in.at[s], ret_recv.at[s]).wait()
        got = ret_in[s]
        dims = (((1,), (1,)), ((), ()))
        cols = slice(s * LANES, (s + 1) * LANES)
        part0 += lax.dot_general(pick0[:, cols], got, dims, preferred_element_type=F32)
        part1 += lax.dot_general(pick1[:, cols], got, dims, preferred_element_type=F32)
    out_ref[...] = (part0 * weight[:, 0:1] + part1 * weight[:, 1:2]).astype(BF)

    sent = pl.ds(0, n_exp - 1)
    pltpu.make_async_copy(disp_out.at[sent], disp_out.at[sent], disp_send).wait()
    pltpu.make_async_copy(ret_out.at[sent], ret_out.at[sent], ret_send).wait()
    for st in range(4):
        for buf, sem in ((x_buf, ag_send), (o_buf, rs_send)):
            most = buf.at[st, pl.ds(0, NY - 1)]
            rest = buf.at[st, NY - 1, pl.ds(0, (NX - 1) * width)]
            pltpu.make_async_copy(most, most, sem.at[st]).wait()
            pltpu.make_async_copy(rest, rest, sem.at[st]).wait()


def shards(tokens, routes, scores, gate_weight, up_weight, down_weight):
    n_exp = lax.axis_size("expert")
    rows, width = tokens.shape
    _, feats, hidden = gate_weight.shape
    cap = 3 * rows // n_exp
    group = n_exp // 4
    span = group * cap
    split = (NX, NY, width, hidden)
    dma = pltpu.SemaphoreType.DMA
    vmem = pl.BlockSpec(memory_space=pltpu.VMEM)
    hbm = pl.BlockSpec(memory_space=pl.ANY)
    return pl.pallas_call(
        moe_kernel,
        out_shape=jax.ShapeDtypeStruct((rows, width), BF),
        in_specs=[vmem, vmem, vmem, hbm, hbm, hbm],
        out_specs=vmem,
        scratch_shapes=[
            pltpu.VMEM(split, BF),
            pltpu.VMEM(split, BF),
            pltpu.VMEM((hidden, feats), BF),
            pltpu.VMEM((NY, 2 * hidden, NX * width), BF),
            pltpu.VMEM((NY, NX * width, hidden), BF),
            pltpu.VMEM((group * LANES, span), BF),
            pltpu.VMEM((n_exp, width, LANES), BF),
            pltpu.VMEM((n_exp, width, LANES), BF),
            pltpu.VMEM((4, NY, NX * width, span), BF),
            pltpu.VMEM((4, 2 * hidden, span), F32),
            pltpu.VMEM((4, hidden, span), BF),
            pltpu.VMEM((4, NY, NX * width, span), BF),
            pltpu.VMEM((4, NY, NX * width, span), BF),
            pltpu.VMEM((4, NY, width, span), BF),
            pltpu.VMEM((n_exp, width, LANES), BF),
            pltpu.VMEM((n_exp, width, LANES), BF),
            pltpu.VMEM((rows, n_exp * LANES), BF),
            pltpu.VMEM((rows, n_exp * LANES), BF),
            dma((3,)), dma, dma((n_exp,)),
            dma((4,)), dma((4, NX, NY)),
            dma((4,)), dma((4, NX, NY)), dma((4, NY)),
            dma, dma((n_exp,)),
        ],
        compiler_params=pltpu.CompilerParams(
            collective_id=0, has_side_effects=True, vmem_limit_bytes=60 * 1024 * 1024),
    )(
        tokens, routes, scores,
        gate_weight[0].reshape(split), up_weight[0].reshape(split), down_weight[0],
    )


def solution(mesh):
    return jax.shard_map(
        shards,
        mesh=mesh,
        in_specs=(
            P("expert", "dp"),
            P("expert", None),
            P("expert", None),
            P("expert", None, "dp"),
            P("expert", None, "dp"),
            P("expert", "dp", None),
        ),
        out_specs=P("expert", "dp"),
        check_vma=False,
    )
```

time: 415 us -> 133 us (0.32)
  waiting for transfers between devices: 324 us -> 0 us
  Pallas kernels: 0 us -> 128 us
  blocking collectives: 23.3 us -> 0 us
  matrix products: 19.8 us -> 0 us
  between operations: 13.5 us -> 0.01 us
  starting transfers between devices: 11.7 us -> 0 us
  local copies, waits for them, and re-layouts: 16 us -> 4.93 us
  other arithmetic: 5.85 us -> 0 us
    unnamed x3 -> x0, waiting for transfers between devices: 223 us -> none
    pallas_call x0 -> x1, Pallas kernels: none -> 128 us  [shards(): pl.pallas_call(moe_kernel, out_shape=jax.ShapeDtypeStruct((rows, width),...]
    all_gather x1 -> x0, waiting for transfers between devices: 89.9 us -> none  [shards(): piece = lax.all_gather(arrived, 'dp', axis=1, tiled=True)]
    all_to_all x1 -> x0, blocking collectives: 23.3 us -> none  [shards(): lax.all_to_all(outgoing.reshape(expert_count, capacity, local_cols), 'exp...]
    dot_general x3 -> x0, matrix products: 19.8 us -> none  [the longest x1 12.3 us: shards(): lax.dot_general(down_mat, hidden, (((0,), (1,)), ((), ())), preferred_ele...]
    all_to_all x1 -> x0, waiting for transfers between devices: 11.7 us -> none  [shards(): lax.all_to_all(summed.reshape(local_cols, expert_count, capacity).astype(...]
    all_to_all x1 -> x0, starting transfers between devices: 11.6 us -> none  [shards(): lax.all_to_all(summed.reshape(local_cols, expert_count, capacity).astype(...]
    unnamed x8 -> x7, local copies, waits for them, and re-layouts: 10.5 us -> 3.31 us
  transfers between devices with their start and end apart: 3 -> 0, of which waited for: 3 -> 0; matrix products, arithmetic and copies ran while one was open for 0% -> 0% of each run, Pallas kernels for 0% -> 0%
where the time goes in v1:
time: 133 us
  Pallas kernels  128 us (96%)
  local copies, waits for them, and re-layouts  4.93 us (4%)
    pallas_call x1, Pallas kernels, shards(): pl.pallas_call(moe_kernel, out_shape=jax.ShapeDtypeStruct((rows, width),...  128 us
    unnamed x7, local copies, waits for them, and re-layouts  3.31 us

profile of v1, /device:TPU:1, one launch (start us, length us, event | category | flops | bytes accessed | tf_op | source)
XLA Modules:
  0.0 133.0 jit_solution(1370914167478791956)
XLA Ops:
  0.0 0.0 copy-start
  0.0 1.6 %copy.7.tokens_ref = bf16[512,64]{1,0:T(8,128)(2,1)} copy(bf16[512,64]{0,1:T(8,128)(2,1)} %param.6) | data formatting | bytes 131072 | tf_op args[0]
  1.6 0.0 copy-done
  1.6 0.0 copy-start.1
  1.6 0.8 copy.8.routes_ref
  2.5 0.0 copy-done.1
  2.5 0.8 copy.9.scores_ref
  3.3 128.1 %shard_map.64 = bf16[512,64]{1,0:T(8,128)(2,1)} custom-call(bf16[512,64]{1,0:T(8,128)(2,1)} %copy.7.tokens_ref, s32[512,2]{1,0:T(8,128)} %copy.8.routes_ref, s32[512,2]{1,0:T(8,128)} %copy.9.scores_ref, bf16[4,8,64,256]{3,2,1,0:T(8,128)(2,1)} %bitcast.3, bf16[4,8,64,256]{3,2,1,0:T(8,128)(2,1)} %bitcast.4, bf16[256,2048]{1,0:T(8,128)(2,1)} %bitcast.5), custom_call_target="tpu_custom_call" | custom-call | tf_op jit(solution)/shard_map/pallas_call | solution.py:290
  131.4 1.6 %copy.10 = bf16[512,64]{0,1:T(8,128)(2,1)} copy(bf16[512,64]{1,0:T(8,128)(2,1)} %shard_map.64) | data formatting | bytes 131072 | tf_op jit(solution)/shard_map/pallas_call | solution.py:290
Async XLA Ops:
  0.0 1.6 %copy-start = (s32[512,2]{0,1:T(2,128)S(1)}, s32[512,2]{0,1:T(2,128)}, u32[]{:S(2)}) copy-start(s32[512,2]{0,1:T(2,128)} %param.7) | copy-start | bytes 12292
  1.6 0.8 copy-start.1

commit v2 on v1

--- a/solution.py
+++ b/solution.py
@@ -20,7 +20,7 @@
     load_sem, disp_send, disp_recv, ag_send, ag_recv, rs_send, rs_recv, turn_recv, ret_send, ret_recv,
 ):
     n_exp = disp_in.shape[0]
-    rows, width = tokens_ref.shape
+    width, rows = tokens_ref.shape
     group = n_exp // 4
     span = x_buf.shape[3]
     cap = span // group
@@ -45,31 +45,25 @@
     for p in range(1, n_exp):
         pl.semaphore_signal(barrier, inc=1, device_id=(dp, lax.rem(me + p, n_exp)), device_id_type=MESH)
 
-    routes = routes_ref[...]
-    first, second = routes[:, 0:1], routes[:, 1:2]
-    lane = lax.broadcasted_iota(jnp.int32, (rows, LANES), 1)
-    is_first = (lane == first).astype(F32)
-    is_second = (lane == second).astype(F32)
+    first, second = routes_ref[0:1, :], routes_ref[1:2, :]
+    expert_at = lax.broadcasted_iota(jnp.int32, (n_exp, rows), 0)
+    is_first = (expert_at == first).astype(F32)
+    is_second = (expert_at == second).astype(F32)
     earlier_mask = (
-        lax.broadcasted_iota(jnp.int32, (rows, rows), 1) < lax.broadcasted_iota(jnp.int32, (rows, rows), 0)
+        lax.broadcasted_iota(jnp.int32, (rows, rows), 0) < lax.broadcasted_iota(jnp.int32, (rows, rows), 1)
     ).astype(F32).astype(BF)
-    earlier = jnp.dot(earlier_mask, (is_first + is_second).astype(BF), preferred_element_type=F32)
-    rank0 = jnp.sum(is_first * earlier, axis=1, keepdims=True).astype(jnp.int32)
-    rank1 = jnp.sum(is_second * earlier, axis=1, keepdims=True).astype(jnp.int32)
-    slot0 = first * LANES + rank0
-    slot1 = second * LANES + rank1
+    earlier = jnp.dot((is_first + is_second).astype(BF), earlier_mask, preferred_element_type=F32)
+    slot0 = first * LANES + jnp.sum(is_first * earlier, axis=0, keepdims=True).astype(jnp.int32)
+    slot1 = second * LANES + jnp.sum(is_second * earlier, axis=0, keepdims=True).astype(jnp.int32)
 
     tok = tokens_ref[...]
     wide = group * LANES
+    slot_at = lax.broadcasted_iota(jnp.int32, (wide, rows), 0)
+    last_dims = (((1,), (1,)), ((), ()))
     for q in range(4):
-        ids = lax.broadcasted_iota(jnp.int32, (rows, wide), 1) + q * wide
-        p0 = (ids == slot0).astype(F32)
-        p1 = (ids == slot1).astype(F32)
-        pick0[:, q * wide:(q + 1) * wide] = p0.astype(BF)
-        pick1[:, q * wide:(q + 1) * wide] = p1.astype(BF)
-        packed = lax.dot_general(
-            tok, (p0 + p1).astype(BF), (((0,), (0,)), ((), ())), preferred_element_type=F32
-        ).astype(BF)
+        ids = slot_at + q * wide
+        picked = ((ids == slot0) | (ids == slot1)).astype(F32).astype(BF)
+        packed = lax.dot_general(tok, picked, last_dims, preferred_element_type=F32).astype(BF)
         for i in range(group):
             disp_out[q * group + i] = packed[:, i * LANES:(i + 1) * LANES]
     disp_in[me] = disp_out[me]
@@ -92,21 +86,23 @@
     for st in range(4):
         acc[st] = jnp.zeros(acc.shape[1:], F32)
 
-    for load in loads:
-        load.wait()
-
-    @pl.loop(0, NY)
-    def _(yy):
+    for q in range(4):
+        ids = slot_at + q * wide
+        pick0[q * wide:(q + 1) * wide, :] = (ids == slot0).astype(F32).astype(BF)
+        pick1[q * wide:(q + 1) * wide, :] = (ids == slot1).astype(F32).astype(BF)
+
+    def turn_gate_up(yy):
         g = gate_raw[:, yy].reshape(NX * width, hidden)
         u = up_raw[:, yy].reshape(NX * width, hidden)
         gu_t[yy, 0:hidden, :] = g.T
         gu_t[yy, hidden:2 * hidden, :] = u.T
 
-    for c in range(NX * NY // 2):
-        turned = down_raw[:, c * LANES:(c + 1) * LANES].T
-        for h in range(2):
-            xx, yy = (2 * c + h) // NY, (2 * c + h) % NY
-            down_t[yy, xx * width:(xx + 1) * width, :] = turned[h * width:(h + 1) * width, :]
+    def turn_down(c):
+        turned = down_raw[:, pl.ds(pl.multiple_of(c * LANES, LANES), LANES)].T
+        for h in range(LANES // width):
+            block = c * (LANES // width) + h
+            xx, yy = block // NY, block % NY
+            down_t[yy, pl.ds(pl.multiple_of(xx * width, width), width), :] = turned[h * width:(h + 1) * width, :]
 
     streams = [(True, 1), (True, -1), (False, 1), (False, -1)]
 
@@ -140,6 +136,13 @@
             packed, sel[...], preferred_element_type=F32).astype(BF)
         ag_copy(st, sign, 0, 0, True).start()
         ag_copy(st, sign, 0, 0, False).start()
+
+    for load in loads:
+        load.wait()
+
+    @pl.loop(0, NY // 2)
+    def _(yy):
+        turn_gate_up(yy)
 
     @pl.loop(1, NX + NY - 1)
     def _(r):
@@ -167,6 +170,11 @@
                         def _():
                             ag_copy(st, sign, j, k, False).start()
 
+        @pl.when(r < NX - 1)
+        def _():
+            for h in range(2):
+                turn_gate_up(NY // 2 + 2 * (r - 1) + h)
+
         done = r - (NX - 1)
 
         @pl.when(done >= 0)
@@ -174,6 +182,8 @@
             for st, (y_first, sign) in enumerate(streams):
                 _, py = where(sign, 0, done)
                 acc[st] += jnp.dot(gu_t[py], x_buf[st, py], preferred_element_type=F32)
+            for h in range(2):
+                turn_down(2 * done + h)
 
     for st in range(4):
         gate = acc[st, 0:hidden, :]
@@ -242,28 +252,30 @@
 
     for st, (y_first, sign) in enumerate(streams):
         total = piece(o_buf, st, sign, 0, 0)[...]
-        spread = lax.dot_general(
-            total, sel[...], (((1,), (1,)), ((), ())), preferred_element_type=F32).astype(BF)
+        spread = lax.dot_general(total, sel[...], last_dims, preferred_element_type=F32).astype(BF)
         for i in range(group):
-            ret_out[st * group + i] = spread[:, i * LANES:(i + 1) * LANES]
+            dest = st * group + i
+            ret_out[dest] = spread[:, i * LANES:(i + 1) * LANES]
+
+            @pl.when(dest != me)
+            def _():
+                ret_copy(dest, me).start()
     ret_in[me] = ret_out[me]
-    for p in range(1, n_exp):
-        ret_copy(lax.rem(me + p, n_exp), me).start()
 
     weight = scores_ref[...].astype(F32)
-    weight = weight / (weight[:, 0:1] + weight[:, 1:2])
-    part0 = jnp.zeros((rows, width), F32)
-    part1 = jnp.zeros((rows, width), F32)
-    for s in range(n_exp):
-        @pl.when(s != me)
-        def _():
-            pltpu.make_async_copy(ret_in.at[s], ret_in.at[s], ret_recv.at[s]).wait()
-        got = ret_in[s]
-        dims = (((1,), (1,)), ((), ()))
-        cols = slice(s * LANES, (s + 1) * LANES)
-        part0 += lax.dot_general(pick0[:, cols], got, dims, preferred_element_type=F32)
-        part1 += lax.dot_general(pick1[:, cols], got, dims, preferred_element_type=F32)
-    out_ref[...] = (part0 * weight[:, 0:1] + part1 * weight[:, 1:2]).astype(BF)
+    weight = weight / (weight[0:1, :] + weight[1:2, :])
+    part0 = jnp.zeros((width, rows), F32)
+    part1 = jnp.zeros((width, rows), F32)
+    for q in range(4):
+        for s in range(q * group, (q + 1) * group):
+            @pl.when(s != me)
+            def _():
+                pltpu.make_async_copy(ret_in.at[s], ret_in.at[s], ret_recv.at[s]).wait()
+        got = jnp.concatenate([ret_in[q * group + i] for i in range(group)], axis=1)
+        cut = slice(q * wide, (q + 1) * wide)
+        part0 += jnp.dot(got, pick0[cut, :], preferred_element_type=F32)
+        part1 += jnp.dot(got, pick1[cut, :], preferred_element_type=F32)
+    out_ref[...] = (part0 * weight[0:1, :] + part1 * weight[1:2, :]).astype(BF)
 
     sent = pl.ds(0, n_exp - 1)
     pltpu.make_async_copy(disp_out.at[sent], disp_out.at[sent], disp_send).wait()
@@ -289,7 +301,7 @@
     hbm = pl.BlockSpec(memory_space=pl.ANY)
     return pl.pallas_call(
         moe_kernel,
-        out_shape=jax.ShapeDtypeStruct((rows, width), BF),
+        out_shape=jax.ShapeDtypeStruct((width, rows), BF),
         in_specs=[vmem, vmem, vmem, hbm, hbm, hbm],
         out_specs=vmem,
         scratch_shapes=[
@@ -309,8 +321,8 @@
             pltpu.VMEM((4, NY, width, span), BF),
             pltpu.VMEM((n_exp, width, LANES), BF),
             pltpu.VMEM((n_exp, width, LANES), BF),
-            pltpu.VMEM((rows, n_exp * LANES), BF),
-            pltpu.VMEM((rows, n_exp * LANES), BF),
+            pltpu.VMEM((n_exp * LANES, rows), BF),
+            pltpu.VMEM((n_exp * LANES, rows), BF),
             dma((3,)), dma, dma((n_exp,)),
             dma((4,)), dma((4, NX, NY)),
             dma((4,)), dma((4, NX, NY)), dma((4, NY)),
@@ -319,9 +331,9 @@
         compiler_params=pltpu.CompilerParams(
             collective_id=0, has_side_effects=True, vmem_limit_bytes=60 * 1024 * 1024),
     )(
-        tokens, routes, scores,
+        tokens.T, routes.T, scores.T,
         gate_weight[0].reshape(split), up_weight[0].reshape(split), down_weight[0],
-    )
+    ).T
 
 
 def solution(mesh):

time: 133 us -> 128 us (0.962)
  local copies, waits for them, and re-layouts: 4.93 us -> 1.47 us
  Pallas kernels: 128 us -> 126 us
    pallas_call x1, Pallas kernels: 128 us -> 126 us  [shards(): pl.pallas_call(moe_kernel, out_shape=jax.ShapeDtypeStruct((width, rows),...]
    unnamed x7 -> x1, local copies, waits for them, and re-layouts: 3.31 us -> 1.47 us
    pallas_call x1 -> x0, local copies, waits for them, and re-layouts: 1.62 us -> none  [shards(): pl.pallas_call(moe_kernel, out_shape=jax.ShapeDtypeStruct((rows, width),...]
where the time goes in v2:
time: 128 us; the launch traced here: 127 us
  Pallas kernels  126 us (98%)
  local copies, waits for them, and re-layouts  1.47 us (1%)
    pallas_call x1, Pallas kernels, shards(): pl.pallas_call(moe_kernel, out_shape=jax.ShapeDtypeStruct((width, rows),...  126 us

profile of v2, /device:TPU:1, one launch (start us, length us, event | category | flops | bytes accessed | tf_op | source)
XLA Modules:
  0.0 127.3 jit_solution(2134363823468081566)
XLA Ops:
  0.0 125.8 %shard_map.64 = bf16[64,512]{1,0:T(8,128)(2,1)} custom-call(bf16[64,512]{1,0:T(8,128)(2,1)} %bitcast.11, s32[2,512]{1,0:T(2,128)} %bitcast.12, s32[2,512]{1,0:T(2,128)} %bitcast.13, bf16[4,8,64,256]{3,2,1,0:T(8,128)(2,1)} %bitcast.7, bf16[4,8,64,256]{3,2,1,0:T(8,128)(2,1)} %bitcast.8, bf16[256,2048]{1,0:T(8,128)(2,1)} %bitcast.9), custom_call_target="tpu_custom_call" | custom-call | tf_op jit(solution)/shard_map/pallas_call | solution.py:302
  125.9 1.5 %copy.8 = bf16[512,64]{0,1:T(8,128)(2,1)} copy(bf16[512,64]{0,1:T(8,128)(2,1)} %bitcast.10) | data formatting | bytes 131072

commit v3 on v2

v3 whole, which is shorter than its diff:
```python
import functools

import jax
import jax.numpy as jnp
from jax import lax
from jax.experimental import pallas as pl
from jax.experimental.pallas import tpu as pltpu
from jax.sharding import PartitionSpec as P

MESH = pl.DeviceIdType.MESH
NX, NY = 4, 8
LANES = 128
BF, F32 = jnp.bfloat16, jnp.float32


OUT_ORDER = (0, 1, 3, 2)
BACK_ORDER = (2, 1, 3, 0)


def moe_kernel(
    tokens_ref, routes_ref, scores_ref, gate_hbm, up_hbm, down_hbm, out_ref,
    gate_w, up_w, down_w, down_t, sel, disp_out, disp_in,
    x_side, x_buf, acc, hid, o_buf, r_main, r_turn, ret_out, ret_in, pick0, pick1,
    load_sem, w_send, w_recv, down_recv, disp_send, disp_recv, side_send, ag_send, ag_recv,
    rs_send, rs_recv, turn_recv, ret_send, ret_recv,
):
    n_exp = disp_in.shape[0]
    width, rows = tokens_ref.shape
    group = n_exp // 4
    span = x_buf.shape[3]
    cap = span // group
    hidden = gate_hbm.shape[3]
    half = hidden // 2
    feats = NX * width
    dp = lax.axis_index("dp")
    me = lax.axis_index("expert")
    x, y = dp // NY, dp % NY
    parity = x % 2
    signs = (1, -1)

    def at_xy(px, py):
        return (lax.rem(px + NX, NX) * NY + lax.rem(py + NY, NY), me)

    own_cols = pl.ds(0, hidden)
    loads = [
        pltpu.make_async_copy(gate_hbm, gate_w.at[:, :, :, own_cols], load_sem.at[0]),
        pltpu.make_async_copy(up_hbm, up_w.at[:, :, :, own_cols], load_sem.at[1]),
        pltpu.make_async_copy(down_hbm, down_w.at[own_cols], load_sem.at[2]),
    ]
    for load in loads:
        load.start()

    barrier = pltpu.get_barrier_semaphore()
    for target in (at_xy(x + 1, y), at_xy(x - 1, y), at_xy(x + 2, y), at_xy(x, y + 1), at_xy(x, y - 1)):
        pl.semaphore_signal(barrier, inc=1, device_id=target, device_id_type=MESH)
    for p in range(1, n_exp):
        pl.semaphore_signal(barrier, inc=1, device_id=(dp, lax.rem(me + p, n_exp)), device_id_type=MESH)

    first, second = routes_ref[0:1, :], routes_ref[1:2, :]
    expert_at = lax.broadcasted_iota(jnp.int32, (n_exp, rows), 0)
    is_first = (expert_at == first).astype(F32)
    is_second = (expert_at == second).astype(F32)
    earlier_mask = (
        lax.broadcasted_iota(jnp.int32, (rows, rows), 0) < lax.broadcasted_iota(jnp.int32, (rows, rows), 1)
    ).astype(F32).astype(BF)
    earlier = jnp.dot((is_first + is_second).astype(BF), earlier_mask, preferred_element_type=F32)
    slot0 = first * LANES + jnp.sum(is_first * earlier, axis=0, keepdims=True).astype(jnp.int32)
    slot1 = second * LANES + jnp.sum(is_second * earlier, axis=0, keepdims=True).astype(jnp.int32)

    tok = tokens_ref[...]
    wide = group * LANES
    slot_at = lax.broadcasted_iota(jnp.int32, (wide, rows), 0)
    last_dims = (((1,), (1,)), ((), ()))
    for q in range(4):
        ids = slot_at + q * wide
        picked = ((ids == slot0) | (ids == slot1)).astype(F32).astype(BF)
        packed = lax.dot_general(tok, picked, last_dims, preferred_element_type=F32).astype(BF)
        for i in range(group):
            disp_out[q * group + i] = packed[:, i * LANES:(i + 1) * LANES]
    disp_in[me] = disp_out[me]

    pl.semaphore_wait(barrier, 5 + n_exp - 1)

    def disp_copy(dest, src):
        return pltpu.make_async_remote_copy(
            src_ref=disp_out.at[dest], dst_ref=disp_in.at[src], send_sem=disp_send, recv_sem=disp_recv.at[src],
            device_id=(dp, dest), device_id_type=MESH)

    for p in range(1, n_exp):
        disp_copy(lax.rem(me + p, n_exp), me).start()

    def sides():
        return ((0, 1, half, hidden), (1, -1, 0, hidden + half))

    def send_gate_up(back):
        yy = lax.rem(y + back + NY, NY)
        for side, step, src, dst in sides():
            for mat, (hbm, buf) in enumerate(((gate_hbm, gate_w), (up_hbm, up_w))):
                pltpu.make_async_remote_copy(
                    src_ref=hbm.at[:, yy, :, pl.ds(src, half)], dst_ref=buf.at[:, yy, :, pl.ds(dst, half)],
                    send_sem=w_send.at[mat], recv_sem=w_recv.at[mat, side, yy],
                    device_id=at_xy(x + step, y), device_id_type=MESH).start()

    def wait_gate_up(back):
        yy = lax.rem(y + back + NY, NY)
        for side, step, src, dst in sides():
            for mat, buf in enumerate((gate_w, up_w)):
                ref = buf.at[:, yy, :, pl.ds(dst, half)]
                pltpu.make_async_copy(ref, ref, w_recv.at[mat, side, yy]).wait()

    def send_down():
        for side, step, src, dst in sides():
            pltpu.make_async_remote_copy(
                src_ref=down_hbm.at[pl.ds(src, half)], dst_ref=down_w.at[pl.ds(dst, half)],
                send_sem=w_send.at[2], recv_sem=down_recv.at[side],
                device_id=at_xy(x + step, y), device_id_type=MESH).start()

    send_gate_up(0)
    send_gate_up(1)
    send_gate_up(-1)

    si = lax.broadcasted_iota(jnp.int32, (wide, span), 0)
    sl = lax.broadcasted_iota(jnp.int32, (wide, span), 1)
    rank_in = si % LANES
    sel[...] = ((sl == (si // LANES) * cap + rank_in) & (rank_in < cap)).astype(F32).astype(BF)

    for st in range(2):
        for mat in range(2):
            acc[st, mat] = jnp.zeros(acc.shape[2:], F32)

    for q in range(4):
        ids = slot_at + q * wide
        pick0[q * wide:(q + 1) * wide, :] = (ids == slot0).astype(F32).astype(BF)
        pick1[q * wide:(q + 1) * wide, :] = (ids == slot1).astype(F32).astype(BF)

    def piece(buf, st, i, k):
        px = lax.rem(x + i, NX)
        py = lax.rem(y - signs[st] * k + 2 * NY, NY)
        return buf.at[st, py, pl.ds(pl.multiple_of(px * width, width), width)]

    def arrive(quarter):
        for i in range(group):
            s = quarter * group + i

            @pl.when(s != me)
            def _():
                pltpu.make_async_copy(disp_in.at[s], disp_in.at[s], disp_recv.at[s]).wait()
        packed = jnp.concatenate([disp_in[quarter * group + i] for i in range(group)], axis=1)
        return jnp.dot(packed, sel[...], preferred_element_type=F32).astype(BF)

    def ag_wait(st, i, k):
        ref = piece(x_buf, st, i, k)
        pltpu.make_async_copy(ref, ref, ag_recv.at[st, k, i]).wait()

    def ag_forward(st, i, k):
        ref = piece(x_buf, st, i, k)
        pltpu.make_async_remote_copy(
            src_ref=ref, dst_ref=ref, send_sem=ag_send.at[st], recv_sem=ag_recv.at[st, k + 1, i],
            device_id=at_xy(x, y + signs[st]), device_id_type=MESH).start()

    def side_copy(src, st, step):
        return pltpu.make_async_remote_copy(
            src_ref=src, dst_ref=piece(x_buf, st, 0, 0), send_sem=side_send.at[st],
            recv_sem=ag_recv.at[st, 0, (NX - step) % NX],
            device_id=at_xy(x + step, y), device_id_type=MESH)

    for st in range(2):
        own = piece(x_buf, st, 0, 0)
        own[...] = arrive(2 * parity + st)
        side_copy(own, st, 2).start()
        ag_forward(st, 0, 0)
    for st in range(2):
        x_side[st] = arrive(2 * (1 - parity) + st)
        side_copy(x_side.at[st], st, 1).start()
        side_copy(x_side.at[st], st, 3).start()
    for load in loads:
        load.wait()
    for i in OUT_ORDER[1:]:
        for st in range(2):
            ag_wait(st, i, 0)
            ag_forward(st, i, 0)
    send_gate_up(2)
    send_gate_up(-2)

    def grow(st, mat, k):
        py = lax.rem(y - signs[st] * k + 2 * NY, NY)
        weights = (gate_w, up_w)[mat][:, py].reshape(feats, 2 * hidden)
        acc[st, mat] += lax.dot_general(
            x_buf[st, py], weights, (((0,), (0,)), ((), ())), preferred_element_type=F32)

    def turn_down(c, rows_from):
        turned = down_w[rows_from:rows_from + hidden, pl.ds(pl.multiple_of(c * LANES, LANES), LANES)].T
        for h in range(LANES // width):
            block = c * (LANES // width) + h
            xx, yy = block // NY, block % NY
            down_t[yy, pl.ds(pl.multiple_of(xx * width, width), width), rows_from:rows_from + hidden] = (
                turned[h * width:(h + 1) * width, :])

    col_blocks = NX * NY * width // LANES

    @pl.loop(1, NY)
    def _(k):
        @pl.when(k == NY - 1)
        def _():
            for side, step, src, dst in sides():
                ref = down_w.at[pl.ds(dst, half)]
                pltpu.make_async_copy(ref, ref, down_recv.at[side]).wait()

            @pl.loop(0, col_blocks)
            def _(c):
                turn_down(c, hidden)

        for n, i in enumerate(OUT_ORDER):
            for st in range(2):
                ag_wait(st, i, k)

                @pl.when(k < NY - 1)
                def _():
                    ag_forward(st, i, k)

            if n == 0:
                @pl.when(k - 1 <= NY // 2)
                def _():
                    wait_gate_up(1 - k)
            if n == 2:
                @pl.when((k - 1 >= 1) & (k - 1 < NY // 2))
                def _():
                    wait_gate_up(k - 1)
            grow(n // 2, n % 2, k - 1)

        @pl.when(k == 1)
        def _():
            send_gate_up(3)
            send_gate_up(-3)

        @pl.when(k == 2)
        def _():
            send_gate_up(4)
            send_down()

        @pl.when(k <= 4)
        def _():
            for h in range(col_blocks // 4):
                turn_down((k - 1) * (col_blocks // 4) + h, 0)

    def produce(st, k):
        py = lax.rem(y - signs[st] * k + 2 * NY, NY)
        o_buf[st, py] = lax.dot_general(
            down_t[py], hid[st], last_dims, preferred_element_type=F32).astype(BF)

    def rs_forward(st, i, k):
        pltpu.make_async_remote_copy(
            src_ref=piece(o_buf, st, i, k), dst_ref=piece(r_main, st, i, k), send_sem=rs_send.at[st],
            recv_sem=rs_recv.at[st, k - 1, i], device_id=at_xy(x, y - signs[st]), device_id_type=MESH).start()

    def rs_add(st, i, k):
        got = piece(r_main, st, i, k)
        pltpu.make_async_copy(got, got, rs_recv.at[st, k, i]).wait()
        own = piece(o_buf, st, i, k)
        own[...] = (own[...].astype(F32) + got[...].astype(F32)).astype(BF)

    for st in range(2):
        for mat in range(2):
            grow(st, mat, NY - 1)
        gate = acc[st, 0]
        hid[st] = (gate / (1.0 + jnp.exp(-gate)) * acc[st, 1]).astype(BF)
        produce(st, NY - 1)
        for i in BACK_ORDER:
            rs_forward(st, i, NY - 1)
    for st in range(2):
        produce(st, NY - 2)

    @pl.loop(1, NY - 1)
    def _(r):
        k = NY - 1 - r
        for n, i in enumerate(BACK_ORDER):
            for st in range(2):
                rs_add(st, i, k)
                rs_forward(st, i, k)
            if n < 2:
                produce(n, k - 1)

    for i in BACK_ORDER:
        for st in range(2):
            rs_add(st, i, 0)
            if i > 0:
                pltpu.make_async_remote_copy(
                    src_ref=piece(o_buf, st, i, 0), dst_ref=r_turn.at[st, i - 1], send_sem=rs_send.at[st],
                    recv_sem=turn_recv.at[st, i - 1], device_id=at_xy(x + i, y), device_id_type=MESH).start()

    def ret_copy(dest, src):
        return pltpu.make_async_remote_copy(
            src_ref=ret_out.at[dest], dst_ref=ret_in.at[src], send_sem=ret_send, recv_sem=ret_recv.at[src],
            device_id=(dp, dest), device_id_type=MESH)

    def turn_wait(st, i):
        ref = r_turn.at[st, i - 1]
        pltpu.make_async_copy(ref, ref, turn_recv.at[st, i - 1]).wait()
        return r_turn[st, i - 1].astype(F32)

    def give_back(quarter, total):
        spread = lax.dot_general(total.astype(BF), sel[...], last_dims, preferred_element_type=F32).astype(BF)
        for i in range(group):
            dest = quarter * group + i
            ret_out[dest] = spread[:, i * LANES:(i + 1) * LANES]

            @pl.when(dest != me)
            def _():
                ret_copy(dest, me).start()

    for st in range(2):
        give_back(2 * parity + st, piece(o_buf, st, 0, 0)[...].astype(F32) + turn_wait(st, 2))
    for st in range(2):
        give_back(2 * (1 - parity) + st, turn_wait(st, 1) + turn_wait(st, 3))
    ret_in[me] = ret_out[me]

    weight = scores_ref[...].astype(F32)
    weight = weight / (weight[0:1, :] + weight[1:2, :])
    part0 = jnp.zeros((width, rows), F32)
    part1 = jnp.zeros((width, rows), F32)
    for q in range(4):
        for s in range(q * group, (q + 1) * group):
            @pl.when(s != me)
            def _():
                pltpu.make_async_copy(ret_in.at[s], ret_in.at[s], ret_recv.at[s]).wait()
        got = jnp.concatenate([ret_in[q * group + i] for i in range(group)], axis=1)
        cut = slice(q * wide, (q + 1) * wide)
        part0 += jnp.dot(got, pick0[cut, :], preferred_element_type=F32)
        part1 += jnp.dot(got, pick1[cut, :], preferred_element_type=F32)
    out_ref[...] = (part0 * weight[0:1, :] + part1 * weight[1:2, :]).astype(BF)

    def drained(ref, sem):
        pltpu.make_async_copy(ref, ref, sem).wait()

    sent = pl.ds(0, n_exp - 1)
    drained(disp_out.at[sent], disp_send)
    drained(ret_out.at[sent], ret_send)
    drained(gate_w.at[:, :, :, own_cols], w_send.at[0])
    drained(up_w.at[:, :, :, own_cols], w_send.at[1])
    drained(down_w.at[own_cols], w_send.at[2])
    for st in range(2):
        drained(x_buf.at[st, 0, pl.ds(0, 3 * width)], side_send.at[st])
        drained(x_buf.at[st, pl.ds(0, NY - 1)], ag_send.at[st])
        drained(o_buf.at[st, pl.ds(0, NY - 1)], rs_send.at[st])
        drained(o_buf.at[st, 0, pl.ds(0, 3 * width)], rs_send.at[st])


def shards(tokens, routes, scores, gate_weight, up_weight, down_weight):
    n_exp = lax.axis_size("expert")
    rows, width = tokens.shape
    _, feats, hidden = gate_weight.shape
    cap = 3 * rows // n_exp
    group = n_exp // 4
    span = group * cap
    split = (NX, NY, width, hidden)
    both = (NX, NY, width, 2 * hidden)
    pieces = (2, NY, NX * width, span)
    dma = pltpu.SemaphoreType.DMA
    vmem = pl.BlockSpec(memory_space=pltpu.VMEM)
    hbm = pl.BlockSpec(memory_space=pl.ANY)
    return pl.pallas_call(
        moe_kernel,
        out_shape=jax.ShapeDtypeStruct((width, rows), BF),
        in_specs=[vmem, vmem, vmem, hbm, hbm, hbm],
        out_specs=vmem,
        scratch_shapes=[
            pltpu.VMEM(both, BF),
            pltpu.VMEM(both, BF),
            pltpu.VMEM((2 * hidden, feats), BF),
            pltpu.VMEM((NY, NX * width, 2 * hidden), BF),
            pltpu.VMEM((group * LANES, span), BF),
            pltpu.VMEM((n_exp, width, LANES), BF),
            pltpu.VMEM((n_exp, width, LANES), BF),
            pltpu.VMEM((2, width, span), BF),
            pltpu.VMEM(pieces, BF),
            pltpu.VMEM((2, 2, span, 2 * hidden), F32),
            pltpu.VMEM((2, span, 2 * hidden), BF),
            pltpu.VMEM(pieces, BF),
            pltpu.VMEM(pieces, BF),
            pltpu.VMEM((2, NX - 1, width, span), BF),
            pltpu.VMEM((n_exp, width, LANES), BF),
            pltpu.VMEM((n_exp, width, LANES), BF),
            pltpu.VMEM((n_exp * LANES, rows), BF),
            pltpu.VMEM((n_exp * LANES, rows), BF),
            dma((3,)), dma((3,)), dma((2, 2, NY)), dma((2,)), dma, dma((n_exp,)),
            dma((2,)), dma((2,)), dma((2, NY, NX)),
            dma((2,)), dma((2, NY, NX)), dma((2, NX - 1)), dma, dma((n_exp,)),
        ],
        compiler_params=pltpu.CompilerParams(
            collective_id=0, has_side_effects=True, vmem_limit_bytes=60 * 1024 * 1024),
    )(
        tokens.T, routes.T, scores.T,
        gate_weight[0].reshape(split), up_weight[0].reshape(split), down_weight[0],
    ).T


def solution(mesh):
    return jax.shard_map(
        shards,
        mesh=mesh,
        in_specs=(
            P("expert", "dp"),
            P("expert", None),
            P("expert", None),
            P("expert", None, "dp"),
            P("expert", None, "dp"),
            P("expert", "dp", None),
        ),
        out_specs=P("expert", "dp"),
        check_vma=False,
    )
```

time: 128 us -> 105 us (0.82)
  Pallas kernels: 126 us -> 104 us
    pallas_call x1, Pallas kernels: 126 us -> 104 us  [shards(): pl.pallas_call(moe_kernel, out_shape=jax.ShapeDtypeStruct((width, rows),...]
where the time goes in v3:
time: 105 us
  Pallas kernels  104 us (99%)
  local copies, waits for them, and re-layouts  1.47 us (1%)
    pallas_call x1, Pallas kernels, shards(): pl.pallas_call(moe_kernel, out_shape=jax.ShapeDtypeStruct((width, rows),...  104 us

profile of v3, /device:TPU:1, one launch (start us, length us, event | category | flops | bytes accessed | tf_op | source)
XLA Modules:
  0.0 105.2 jit_solution(2258727219891917316)
XLA Ops:
  0.0 103.7 %shard_map.64 = bf16[64,512]{1,0:T(8,128)(2,1)} custom-call(bf16[64,512]{1,0:T(8,128)(2,1)} %bitcast.11, s32[2,512]{1,0:T(2,128)} %bitcast.12, s32[2,512]{1,0:T(2,128)} %bitcast.13, bf16[4,8,64,256]{3,2,1,0:T(8,128)(2,1)} %bitcast.7, bf16[4,8,64,256]{3,2,1,0:T(8,128)(2,1)} %bitcast.8, bf16[256,2048]{1,0:T(8,128)(2,1)} %bitcast.9), custom_call_target="tpu_custom_call" | custom-call | tf_op jit(solution)/shard_map/pallas_call | solution.py:361
  103.7 1.5 %copy.8 = bf16[512,64]{0,1:T(8,128)(2,1)} copy(bf16[512,64]{0,1:T(8,128)(2,1)} %bitcast.10) | data formatting | bytes 131072

commit v4 on v3

v4 whole, which is shorter than its diff:
```python
import functools

import jax
import jax.numpy as jnp
from jax import lax
from jax.experimental import pallas as pl
from jax.experimental.pallas import tpu as pltpu
from jax.sharding import PartitionSpec as P

MESH = pl.DeviceIdType.MESH
NX, NY = 4, 8
LANES = 128
BF, F32 = jnp.bfloat16, jnp.float32


OUT_ORDER = ((0, 3, 1, 2), (0, 1, 3, 2))
BACK_ORDER = (2, 1, 3, 0)


def moe_kernel(
    tokens_ref, routes_ref, scores_ref, gate_hbm, up_hbm, down_hbm, out_ref,
    gate_w, up_w, down_w, down_t, sel, disp_out, disp_in,
    x_side, x_relay, x_buf, acc, hid, o_buf, r_main, r_turn, ret_out, ret_in, pick,
    load_sem, w_send, w_recv, down_recv, disp_send, disp_recv, side_send, relay_recv, ag_send, ag_recv,
    rs_send, rs_recv, turn_recv, ret_send, ret_recv,
):
    n_exp = disp_in.shape[0]
    width, rows = tokens_ref.shape
    group = n_exp // 4
    span = x_buf.shape[3]
    fold = span // group // 2
    hidden = gate_hbm.shape[3]
    half = hidden // 2
    feats = NX * width
    dp = lax.axis_index("dp")
    me = lax.axis_index("expert")
    x, y = dp // NY, dp % NY
    parity = x % 2
    signs = (1, -1)

    def at_xy(px, py):
        return (lax.rem(px + NX, NX) * NY + lax.rem(py + NY, NY), me)

    own_cols = pl.ds(0, hidden)
    loads = [
        pltpu.make_async_copy(hbm.at[:, :, :, pl.ds(h * half, half)], buf.at[h], load_sem.at[2 * mat + h])
        for mat, (hbm, buf) in enumerate(((gate_hbm, gate_w), (up_hbm, up_w)))
        for h in range(2)
    ] + [
        pltpu.make_async_copy(down_hbm, down_w.at[own_cols], load_sem.at[4]),
    ]
    for load in loads:
        load.start()

    barrier = pltpu.get_barrier_semaphore()
    for target in (at_xy(x + 1, y), at_xy(x - 1, y), at_xy(x + 2, y), at_xy(x, y + 1), at_xy(x, y - 1)):
        pl.semaphore_signal(barrier, inc=1, device_id=target, device_id_type=MESH)
    for p in range(1, n_exp):
        pl.semaphore_signal(barrier, inc=1, device_id=(dp, lax.rem(me + p, n_exp)), device_id_type=MESH)

    pl.semaphore_wait(barrier, 5 + n_exp - 1)

    def sides():
        return ((0, 1, half, hidden), (1, -1, 0, hidden + half))

    def send_gate_up(back):
        yy = lax.rem(y + back + NY, NY)
        for side, step, src, dst in sides():
            for mat, buf in enumerate((gate_w, up_w)):
                pltpu.make_async_remote_copy(
                    src_ref=buf.at[src // half, :, yy], dst_ref=buf.at[dst // half, :, yy],
                    send_sem=w_send.at[mat], recv_sem=w_recv.at[mat, side, yy],
                    device_id=at_xy(x + step, y), device_id_type=MESH).start()

    def wait_gate_up(back):
        yy = lax.rem(y + back + NY, NY)
        for side, step, src, dst in sides():
            for mat, buf in enumerate((gate_w, up_w)):
                ref = buf.at[dst // half, :, yy]
                pltpu.make_async_copy(ref, ref, w_recv.at[mat, side, yy]).wait()

    def send_down():
        for side, step, src, dst in sides():
            pltpu.make_async_remote_copy(
                src_ref=down_w.at[pl.ds(src, half)], dst_ref=down_w.at[pl.ds(dst, half)],
                send_sem=w_send.at[2], recv_sem=down_recv.at[side],
                device_id=at_xy(x + step, y), device_id_type=MESH).start()

    for load in loads:
        load.wait()
    send_gate_up(0)
    send_gate_up(1)
    send_gate_up(-1)

    first, second = routes_ref[0:1, :], routes_ref[1:2, :]
    expert_at = lax.broadcasted_iota(jnp.int32, (n_exp, rows), 0)
    is_first = (expert_at == first).astype(F32)
    is_second = (expert_at == second).astype(F32)
    earlier_mask = (
        lax.broadcasted_iota(jnp.int32, (rows, rows), 0) < lax.broadcasted_iota(jnp.int32, (rows, rows), 1)
    ).astype(F32).astype(BF)
    named = is_first + is_second
    earlier = jnp.dot(named.astype(BF), earlier_mask, preferred_element_type=F32)
    rank = jnp.where(named > 0.0, earlier, -1.0)

    tok = tokens_ref[...]
    none = jnp.zeros((width, rows), BF)
    tok_pair = jnp.concatenate(
        [jnp.concatenate([tok, none], axis=1), jnp.concatenate([none, tok], axis=1)], axis=0)
    slot_low = lax.broadcasted_iota(jnp.int32, (fold, rows), 0).astype(F32)
    slot_high = (slot_low + fold).astype(BF)
    slot_low = slot_low.astype(BF)
    last_dims = (((1,), (1,)), ((), ()))
    first_dims = (((0,), (0,)), ((), ()))
    for q in range(4):
        for i in range(group):
            e = q * group + i
            of_slot = jnp.tile(jnp.broadcast_to(rank[e:e + 1, :], (16, rows)).astype(BF), (fold // 16, 1))
            pick[e, :, 0:rows] = jnp.where(slot_low == of_slot, 1.0, 0.0).astype(BF)
            pick[e, :, rows:2 * rows] = jnp.where(slot_high == of_slot, 1.0, 0.0).astype(BF)
        picked = pick[q * group:(q + 1) * group].reshape(group * fold, 2 * rows)
        packed = lax.dot_general(picked, tok_pair, last_dims, preferred_element_type=F32).astype(BF)
        disp_out[q * group:(q + 1) * group] = packed.reshape(group, fold, 2 * width)
    disp_in[me] = disp_out[me]

    def disp_copy(dest, src):
        return pltpu.make_async_remote_copy(
            src_ref=disp_out.at[dest], dst_ref=disp_in.at[src], send_sem=disp_send, recv_sem=disp_recv.at[src],
            device_id=(dp, dest), device_id_type=MESH)

    far_first = sorted(range(1, n_exp), key=lambda p: abs(2 * p - n_exp))
    for p in far_first:
        disp_copy(lax.rem(me + p, n_exp), me).start()

    half_span = group * fold
    si = lax.broadcasted_iota(jnp.int32, (half_span, span), 0)
    sl = lax.broadcasted_iota(jnp.int32, (half_span, span), 1)
    sel[:, 0:span] = (sl == si).astype(F32).astype(BF)
    sel[:, span:2 * span] = (sl == si + half_span).astype(F32).astype(BF)

    for st in range(2):
        for mat in range(2):
            acc[st, mat] = jnp.zeros(acc.shape[2:], F32)

    weight = scores_ref[...].astype(F32)
    weight = weight / (weight[0:1, :] + weight[1:2, :])
    share = is_first * weight[0:1, :] + is_second * weight[1:2, :]
    for e in range(n_exp):
        for h in range(2):
            cols = slice(h * rows, (h + 1) * rows)
            pick[e, :, cols] = (pick[e, :, cols].astype(F32) * share[e:e + 1, :]).astype(BF)

    def piece(buf, st, i, k):
        px = lax.rem(x + i, NX)
        py = lax.rem(y - signs[st] * k + 2 * NY, NY)
        return buf.at[st, py, pl.ds(pl.multiple_of(px * width, width), width)]

    def arrive(quarter):
        for i in range(group):
            s = quarter * group + i

            @pl.when(s != me)
            def _():
                pltpu.make_async_copy(disp_in.at[s], disp_in.at[s], disp_recv.at[s]).wait()
        packed = disp_in[pl.ds(quarter * group, group)].reshape(half_span, 2 * width)
        low = lax.dot_general(packed, sel[:, 0:span], first_dims, preferred_element_type=F32)
        high = lax.dot_general(packed, sel[:, span:2 * span], first_dims, preferred_element_type=F32)
        return (low[0:width] + high[width:2 * width]).astype(BF)

    def ag_wait(st, i, k):
        ref = piece(x_buf, st, i, k)
        pltpu.make_async_copy(ref, ref, ag_recv.at[st, k, i]).wait()

    def ag_forward(st, i, k):
        ref = piece(x_buf, st, i, k)
        pltpu.make_async_remote_copy(
            src_ref=ref, dst_ref=ref, send_sem=ag_send.at[st], recv_sem=ag_recv.at[st, k + 1, i],
            device_id=at_xy(x, y + signs[st]), device_id_type=MESH).start()

    def side_copy(src, st, step):
        return pltpu.make_async_remote_copy(
            src_ref=src, dst_ref=piece(x_buf, st, 0, 0), send_sem=side_send.at[st],
            recv_sem=ag_recv.at[st, 0, (NX - step) % NX],
            device_id=at_xy(x + step, y), device_id_type=MESH)

    def relay_out(st):
        return pltpu.make_async_remote_copy(
            src_ref=piece(x_buf, st, 0, 0), dst_ref=x_relay.at[st], send_sem=side_send.at[st],
            recv_sem=relay_recv.at[st], device_id=at_xy(x + signs[st], y), device_id_type=MESH)

    def relay_on(st):
        return pltpu.make_async_remote_copy(
            src_ref=x_relay.at[st], dst_ref=piece(x_buf, st, NX - signs[st], 0), send_sem=side_send.at[st],
            recv_sem=ag_recv.at[st, 0, 2], device_id=at_xy(x + signs[st], y), device_id_type=MESH)

    for st in range(2):
        own = piece(x_buf, st, 0, 0)
        own[...] = arrive(2 * parity + st)
        ag_forward(st, 0, 0)
        relay_out(st).start()
    for st in range(2):
        x_side[st] = arrive(2 * (1 - parity) + st)
    side_copy(x_side.at[0], 0, 1).start()
    side_copy(x_side.at[1], 1, 3).start()
    side_copy(x_side.at[1], 1, 1).start()
    side_copy(x_side.at[0], 0, 3).start()
    for st in range(2):
        pltpu.make_async_copy(x_relay.at[st], x_relay.at[st], relay_recv.at[st]).wait()
        relay_on(st).start()
    for n in range(NX):
        for st in range(2):
            i = OUT_ORDER[st][n]
            k = 1 if i == 0 else 0
            ag_wait(st, i, k)
            ag_forward(st, i, k)
    send_gate_up(2)
    send_gate_up(-2)

    def grow(st, mat, k):
        py = lax.rem(y - signs[st] * k + 2 * NY, NY)
        buf = (gate_w, up_w)[mat]
        weights = jnp.concatenate([buf[b, :, py].reshape(feats, half) for b in range(4)], axis=1)
        acc[st, mat] += lax.dot_general(
            x_buf[st, py], weights, (((0,), (0,)), ((), ())), preferred_element_type=F32)

    def turn_down(c, rows_from):
        turned = down_w[rows_from:rows_from + hidden, pl.ds(pl.multiple_of(c * LANES, LANES), LANES)].T
        for h in range(LANES // width):
            block = c * (LANES // width) + h
            xx, yy = block // NY, block % NY
            down_t[yy, pl.ds(pl.multiple_of(xx * width, width), width), rows_from:rows_from + hidden] = (
                turned[h * width:(h + 1) * width, :])

    col_blocks = NX * NY * width // LANES

    @pl.loop(1, NY)
    def _(k):
        for n in range(NX):
            if n == 2:
                @pl.when(k == NY - 1)
                def _():
                    for side, step, src, dst in sides():
                        ref = down_w.at[pl.ds(dst, half)]
                        pltpu.make_async_copy(ref, ref, down_recv.at[side]).wait()

                    @pl.loop(0, col_blocks)
                    def _(c):
                        turn_down(c, hidden)

            for st in range(2):
                i = OUT_ORDER[st][n]
                if i == 0:
                    @pl.when(k < NY - 1)
                    def _():
                        ag_wait(st, i, k + 1)

                    @pl.when(k < NY - 2)
                    def _():
                        ag_forward(st, i, k + 1)
                else:
                    ag_wait(st, i, k)

                    @pl.when(k < NY - 1)
                    def _():
                        ag_forward(st, i, k)

            if n == 0:
                @pl.when(k - 1 <= NY // 2)
                def _():
                    wait_gate_up(1 - k)
            if n == 2:
                @pl.when((k - 1 >= 1) & (k - 1 < NY // 2))
                def _():
                    wait_gate_up(k - 1)
            grow(n // 2, n % 2, k - 1)

        @pl.when(k == 1)
        def _():
            send_gate_up(3)
            send_gate_up(-3)

        @pl.when(k == 2)
        def _():
            send_gate_up(4)
            send_down()

        @pl.when(k <= 4)
        def _():
            for h in range(col_blocks // 4):
                turn_down((k - 1) * (col_blocks // 4) + h, 0)

    def produce(st, k):
        py = lax.rem(y - signs[st] * k + 2 * NY, NY)
        o_buf[st, py] = lax.dot_general(
            down_t[py], hid[st], last_dims, preferred_element_type=F32).astype(BF)

    def rs_forward(st, i, k):
        pltpu.make_async_remote_copy(
            src_ref=piece(o_buf, st, i, k), dst_ref=piece(r_main, st, i, k), send_sem=rs_send.at[st],
            recv_sem=rs_recv.at[st, k - 1, i], device_id=at_xy(x, y - signs[st]), device_id_type=MESH).start()

    def rs_add(st, i, k):
        got = piece(r_main, st, i, k)
        pltpu.make_async_copy(got, got, rs_recv.at[st, k, i]).wait()
        own = piece(o_buf, st, i, k)
        own[...] = (own[...].astype(F32) + got[...].astype(F32)).astype(BF)

    for st in range(2):
        for mat in range(2):
            grow(st, mat, NY - 1)
        gate = acc[st, 0]
        hid[st] = (gate / (1.0 + jnp.exp(-gate)) * acc[st, 1]).astype(BF)
        produce(st, NY - 1)
        for i in BACK_ORDER:
            rs_forward(st, i, NY - 1)
    for st in range(2):
        produce(st, NY - 2)

    @pl.loop(1, NY - 1)
    def _(r):
        k = NY - 1 - r
        for n, i in enumerate(BACK_ORDER):
            for st in range(2):
                rs_add(st, i, k)
                rs_forward(st, i, k)
            if n < 2:
                produce(n, k - 1)

    for i in BACK_ORDER:
        for st in range(2):
            rs_add(st, i, 0)
            if i > 0:
                pltpu.make_async_remote_copy(
                    src_ref=piece(o_buf, st, i, 0), dst_ref=r_turn.at[st, i - 1], send_sem=rs_send.at[st],
                    recv_sem=turn_recv.at[st, i - 1], device_id=at_xy(x + i, y), device_id_type=MESH).start()

    def ret_copy(dest, src):
        return pltpu.make_async_remote_copy(
            src_ref=ret_out.at[dest], dst_ref=ret_in.at[src], send_sem=ret_send, recv_sem=ret_recv.at[src],
            device_id=(dp, dest), device_id_type=MESH)

    def turn_wait(st, i):
        ref = r_turn.at[st, i - 1]
        pltpu.make_async_copy(ref, ref, turn_recv.at[st, i - 1]).wait()
        return r_turn[st, i - 1].astype(F32)

    def give_back(quarter, total):
        total = total.astype(BF)
        none = jnp.zeros((width, span), BF)
        pair = jnp.concatenate(
            [jnp.concatenate([total, none], axis=1), jnp.concatenate([none, total], axis=1)], axis=0)
        packed = lax.dot_general(sel[...], pair, last_dims, preferred_element_type=F32).astype(BF)
        ret_out[pl.ds(quarter * group, group)] = packed.reshape(group, fold, 2 * width)

    for st in range(2):
        give_back(2 * parity + st, piece(o_buf, st, 0, 0)[...].astype(F32) + turn_wait(st, 2))
    for st in range(2):
        give_back(2 * (1 - parity) + st, turn_wait(st, 1) + turn_wait(st, 3))
    for p in far_first:
        ret_copy(lax.rem(me + p, n_exp), me).start()
    ret_in[me] = ret_out[me]

    combined = jnp.zeros((width, rows), F32)
    for q in range(4):
        for e in range(q * group, (q + 1) * group):
            @pl.when(e != me)
            def _():
                pltpu.make_async_copy(ret_in.at[e], ret_in.at[e], ret_recv.at[e]).wait()
        got = ret_in[q * group:(q + 1) * group].reshape(half_span, 2 * width)
        picked = pick[q * group:(q + 1) * group].reshape(half_span, 2 * rows)
        low = lax.dot_general(got, picked[:, 0:rows], first_dims, preferred_element_type=F32)
        high = lax.dot_general(got, picked[:, rows:2 * rows], first_dims, preferred_element_type=F32)
        combined += low[0:width] + high[width:2 * width]
    out_ref[...] = combined.astype(BF)

    def drained(ref, sem):
        pltpu.make_async_copy(ref, ref, sem).wait()

    sent = pl.ds(0, n_exp - 1)
    drained(disp_out.at[sent], disp_send)
    drained(ret_out.at[sent], ret_send)
    drained(gate_w.at[pl.ds(0, 2)], w_send.at[0])
    drained(up_w.at[pl.ds(0, 2)], w_send.at[1])
    drained(down_w.at[own_cols], w_send.at[2])
    for st in range(2):
        drained(x_buf.at[st, 0], side_send.at[st])
        drained(x_buf.at[st, pl.ds(0, NY - 1)], ag_send.at[st])
        drained(o_buf.at[st, pl.ds(0, NY - 1)], rs_send.at[st])
        drained(o_buf.at[st, 0, pl.ds(0, 3 * width)], rs_send.at[st])


def shards(tokens, routes, scores, gate_weight, up_weight, down_weight):
    n_exp = lax.axis_size("expert")
    rows, width = tokens.shape
    _, feats, hidden = gate_weight.shape
    cap = 3 * rows // n_exp
    group = n_exp // 4
    span = group * cap
    split = (NX, NY, width, hidden)
    both = (4, NX, NY, width, hidden // 2)
    pieces = (2, NY, NX * width, span)
    dma = pltpu.SemaphoreType.DMA
    vmem = pl.BlockSpec(memory_space=pltpu.VMEM)
    hbm = pl.BlockSpec(memory_space=pl.ANY)
    return pl.pallas_call(
        moe_kernel,
        out_shape=jax.ShapeDtypeStruct((width, rows), BF),
        in_specs=[vmem, vmem, vmem, hbm, hbm, hbm],
        out_specs=vmem,
        scratch_shapes=[
            pltpu.VMEM(both, BF),
            pltpu.VMEM(both, BF),
            pltpu.VMEM((2 * hidden, feats), BF),
            pltpu.VMEM((NY, NX * width, 2 * hidden), BF),
            pltpu.VMEM((span // 2, 2 * span), BF),
            pltpu.VMEM((n_exp, cap // 2, 2 * width), BF),
            pltpu.VMEM((n_exp, cap // 2, 2 * width), BF),
            pltpu.VMEM((2, width, span), BF),
            pltpu.VMEM((2, width, span), BF),
            pltpu.VMEM(pieces, BF),
            pltpu.VMEM((2, 2, span, 2 * hidden), F32),
            pltpu.VMEM((2, span, 2 * hidden), BF),
            pltpu.VMEM(pieces, BF),
            pltpu.VMEM(pieces, BF),
            pltpu.VMEM((2, NX - 1, width, span), BF),
            pltpu.VMEM((n_exp, cap // 2, 2 * width), BF),
            pltpu.VMEM((n_exp, cap // 2, 2 * width), BF),
            pltpu.VMEM((n_exp, cap // 2, 2 * rows), BF),
            dma((5,)), dma((3,)), dma((2, 2, NY)), dma((2,)), dma, dma((n_exp,)),
            dma((2,)), dma((2,)), dma((2,)), dma((2, NY, NX)),
            dma((2,)), dma((2, NY, NX)), dma((2, NX - 1)), dma, dma((n_exp,)),
        ],
        compiler_params=pltpu.CompilerParams(
            collective_id=0, has_side_effects=True, vmem_limit_bytes=60 * 1024 * 1024),
    )(
        tokens.T, routes.T, scores.T,
        gate_weight[0].reshape(split), up_weight[0].reshape(split), down_weight[0],
    ).T


def solution(mesh):
    return jax.shard_map(
        shards,
        mesh=mesh,
        in_specs=(
            P("expert", "dp"),
            P("expert", None),
            P("expert", None),
            P("expert", None, "dp"),
            P("expert", None, "dp"),
            P("expert", "dp", None),
        ),
        out_specs=P("expert", "dp"),
        check_vma=False,
    )
```

time: 105 us -> 105 us (level)
  no operation moved by 1% of the time
where the time goes in v4:
time: 105 us
  Pallas kernels  103 us (98%)
  local copies, waits for them, and re-layouts  1.47 us (1%)
    pallas_call x1, Pallas kernels, shards(): pl.pallas_call(moe_kernel, out_shape=jax.ShapeDtypeStruct((width, rows),...  103 us

profile of v4, /device:TPU:1, one launch (start us, length us, event | category | flops | bytes accessed | tf_op | source)
XLA Modules:
  0.0 104.9 jit_solution(11062869353672408632)
XLA Ops:
  0.0 103.5 %shard_map.64 = bf16[64,512]{1,0:T(8,128)(2,1)} custom-call(bf16[64,512]{1,0:T(8,128)(2,1)} %bitcast.11, s32[2,512]{1,0:T(2,128)} %bitcast.12, s32[2,512]{1,0:T(2,128)} %bitcast.13, bf16[4,8,64,256]{3,2,1,0:T(8,128)(2,1)} %bitcast.7, bf16[4,8,64,256]{3,2,1,0:T(8,128)(2,1)} %bitcast.8, bf16[256,2048]{1,0:T(8,128)(2,1)} %bitcast.9), custom_call_target="tpu_custom_call" | custom-call | tf_op jit(solution)/shard_map/pallas_call | solution.py:405
  103.5 1.5 %copy.8 = bf16[512,64]{0,1:T(8,128)(2,1)} copy(bf16[512,64]{0,1:T(8,128)(2,1)} %bitcast.10) | data formatting | bytes 131072

commit v5 on v4

--- a/solution.py
+++ b/solution.py
@@ -207,14 +207,17 @@
     for st in range(2):
         pltpu.make_async_copy(x_relay.at[st], x_relay.at[st], relay_recv.at[st]).wait()
         relay_on(st).start()
+    send_gate_up(2)
+    send_gate_up(-2)
     for n in range(NX):
         for st in range(2):
             i = OUT_ORDER[st][n]
             k = 1 if i == 0 else 0
             ag_wait(st, i, k)
             ag_forward(st, i, k)
-    send_gate_up(2)
-    send_gate_up(-2)
+
+    send_gate_up(3)
+    send_gate_up(-3)
 
     def grow(st, mat, k):
         py = lax.rem(y - signs[st] * k + 2 * NY, NY)
@@ -275,11 +278,6 @@
             grow(n // 2, n % 2, k - 1)
 
         @pl.when(k == 1)
-        def _():
-            send_gate_up(3)
-            send_gate_up(-3)
-
-        @pl.when(k == 2)
         def _():
             send_gate_up(4)
             send_down()

time: 105 us -> 105 us (level)
  no operation moved by 1% of the time
where the time goes in v5:
time: 105 us
  Pallas kernels  103 us (98%)
  local copies, waits for them, and re-layouts  1.47 us (1%)
    pallas_call x1, Pallas kernels, shards(): pl.pallas_call(moe_kernel, out_shape=jax.ShapeDtypeStruct((width, rows),...  103 us

profile of v5, /device:TPU:1, one launch (start us, length us, event | category | flops | bytes accessed | tf_op | source)
XLA Modules:
  0.0 104.9 jit_solution(1065206605937118330)
XLA Ops:
  0.0 103.4 %shard_map.64 = bf16[64,512]{1,0:T(8,128)(2,1)} custom-call(bf16[64,512]{1,0:T(8,128)(2,1)} %bitcast.11, s32[2,512]{1,0:T(2,128)} %bitcast.12, s32[2,512]{1,0:T(2,128)} %bitcast.13, bf16[4,8,64,256]{3,2,1,0:T(8,128)(2,1)} %bitcast.7, bf16[4,8,64,256]{3,2,1,0:T(8,128)(2,1)} %bitcast.8, bf16[256,2048]{1,0:T(8,128)(2,1)} %bitcast.9), custom_call_target="tpu_custom_call" | custom-call | tf_op jit(solution)/shard_map/pallas_call | solution.py:403
  103.4 1.5 %copy.8 = bf16[512,64]{0,1:T(8,128)(2,1)} copy(bf16[512,64]{0,1:T(8,128)(2,1)} %bitcast.10) | data formatting | bytes 131072
